TPU v7x, 256 devices: a whole 4x4x8 slice. The times are simulated.
256 devices in a mesh: dp: 2 (over core), ctx: 16 (over z_hi, y), exp: 8 (over x, z_lo).
Axes of the slice: x: 4, y: 4, z: 8 (z_hi: 4, z_lo: 2; z = z_hi * 2 + z_lo), core: 2. Of those that a mesh axis runs over, the one named last changes fastest.
Arguments:
- tokens: bfloat16 [2, 2048, 2560], P('dp', 'ctx'), may hold values from -6 to 6
- queries: bfloat16 [2, 2048, 16, 576], P('dp', 'ctx', 'exp'), may hold values from -240 to 240
- kv_weight: bfloat16 [2560, 576], P('exp'), may hold values from -0.125 to 0.125
- kv_gain: bfloat16 [512], replicated, may hold values from 0.5 to 1.5
- uv_weight: bfloat16 [16, 512, 128], P('exp'), may hold values from -0.75 to 0.75
- out_weight: bfloat16 [2048, 2560], P('exp'), may hold values from -0.5 to 0.5
- post_gain: bfloat16 [2560], replicated, may hold values from 0.5 to 1.5
- router_weight: bfloat16 [2560, 32], replicated, may hold values from -0.125 to 0.125
- expert_ids: int32 [2, 2048, 6], P('dp', 'ctx'), may hold values from 0 to 31, all different within a row; in each aligned block of 128 rows (0 to 127, 128 to 255, ..., all dimensions but the last counted through in order) at most 32 rows name the same one
- doc_ids: int32 [2, 2048], P('dp', 'ctx'), may hold values from 0 to 3, never falling along the last dimension, each value on 1 to 1024 neighbouring positions
- gate_weight: bfloat16 [32, 2560, 1536], P('ctx', None, 'exp'), may hold values from -0.125 to 0.125
- up_weight: bfloat16 [32, 2560, 1536], P('ctx', None, 'exp'), may hold values from -0.125 to 0.125
- down_weight: bfloat16 [32, 1536, 2560], P('ctx', 'exp'), may hold values from -0.15625 to 0.15625
- cotangent: bfloat16 [2, 2048, 2560], P('dp', 'ctx'), may hold values from -6 to 6
Outputs:
- layer_out: bfloat16 [2, 2048, 2560], P('dp', 'ctx')
- router_grad: float32 [2560, 32], replicated
- gate_grad: bfloat16 [32, 2560, 1536], P('ctx', 'dp', 'exp')
- up_grad: bfloat16 [32, 2560, 1536], P('ctx', 'dp', 'exp')
- down_grad: bfloat16 [32, 1536, 2560], P('ctx', 'exp', 'dp')
Inputs may be any that keep to these rules, and one draw needn't show every extreme that they name: `expert_ids`: in each aligned block of 128 positions of a sequence no expert is named by more than 32 of the block's assignments; the experts of one token differ. `doc_ids`: document numbers never fall along a sequence; a document has at most 1024 positions.
All inputs are finite; a program needn't handle non-finite values.
Results may differ from a plain program's by a relative error of at most 0.023.
The roundings to bfloat16 on the way count: a program that leaves them out, or rounds other values in their place, can miss the bound.
Values may be sent and summed in bfloat16 or wider, within the bound.
No kernel may reach another device: no remote copies, remote signals or barrier semaphores. Data moves between devices by JAX's collectives and lax.ppermute only.
A program may use at most 128 MiB of HBM per device.

v0:
```python
import jax
import jax.numpy as jnp
from jax import lax
from jax.sharding import PartitionSpec as P

ROPE = 64
NOPE = 128
epsilon = 1e-06


def from_everyone(array, axis):
    count = lax.axis_size(axis)
    return lax.all_to_all(
        jnp.broadcast_to(array[None], (count, *array.shape)), axis, 0, 0, tiled=True
    )


def taken_together(array, axis):
    everything = from_everyone(array, axis)
    return jnp.sum(everything, axis=0)


def in_one_piece(arrays, axis, split_dim, concat_dim, along):
    both = jnp.concatenate(arrays, axis=along)
    result, at, gathered = (
        lax.all_to_all(both, axis, split_axis=split_dim, concat_axis=concat_dim, tiled=True),
        0,
        [],
    )
    for a in arrays:
        gathered.append(lax.slice_in_dim(result, at, at + a.shape[along], axis=along))
        at += a.shape[along]
    return tuple(gathered)


def rms_scale(values, gain):
    return values * lax.rsqrt(jnp.mean(values * values, axis=-1, keepdims=True) + epsilon) * gain


def rotate(rope_part, positions):
    half_width = rope_part.shape[-1] // 2
    frequency = jnp.power(
        10000.0, -2.0 * jnp.arange(half_width, dtype=jnp.float32) / rope_part.shape[-1]
    )
    angles = positions.astype(jnp.float32)[:, None] * frequency[None, :]
    cosine = jnp.cos(angles)
    sine_part = jnp.sin(angles)
    first_half = rope_part[:, :half_width]
    second = rope_part[:, half_width:]
    return jnp.concatenate(
        [first_half * cosine - second * sine_part, second * cosine + first_half * sine_part], axis=1
    )


def route_slots(outgoing):
    moved = lax.all_to_all(outgoing, ("dp", "ctx"), split_axis=0, concat_axis=0, tiled=True)
    return moved


def local(
    tokens,
    queries,
    kv_weight,
    kv_gain,
    uv_weight,
    out_weight,
    post_gain,
    router_weight,
    expert_ids,
    doc_ids,
    gate_weight,
    up_weight,
    down_weight,
    cotangent,
):
    local_rows = tokens[0]
    seq_rows = local_rows.shape[0]
    model_width = local_rows.shape[1]
    latent_width = kv_gain.shape[0]
    row_share = kv_weight.shape[0]
    columns = lax.dynamic_slice_in_dim(local_rows, lax.axis_index("exp") * row_share, row_share, 1)
    compressed = taken_together(
        jnp.dot(columns, kv_weight, preferred_element_type=jnp.float32), "exp"
    )
    positions = lax.axis_index("ctx") * seq_rows + jnp.arange(seq_rows, dtype=jnp.int32)
    latent = rms_scale(compressed[:, :latent_width], kv_gain.astype(jnp.float32)).astype(
        jnp.bfloat16
    )
    rope_key = rotate(compressed[:, latent_width:], positions).astype(jnp.bfloat16)
    key_rows = jnp.concatenate([latent, rope_key], axis=1)
    all_keys, all_docs = (
        lax.all_gather(key_rows, "ctx", axis=0, tiled=True),
        lax.all_gather(doc_ids[0], "ctx", axis=0, tiled=True),
    )
    key_positions = jnp.arange(all_keys.shape[0], dtype=jnp.int32)
    allowed = (key_positions[None, :] <= positions[:, None]) & (
        all_docs[None, :] == doc_ids[0][:, None]
    )
    allowed = allowed[:, None, :]
    score_scale = (NOPE + ROPE) ** (-0.5)
    scores = (
        jnp.einsum("qhd,kd->qhk", queries[0], all_keys, preferred_element_type=jnp.float32)
        * score_scale
    )
    score_peak = jnp.max(jnp.where(allowed, scores, -1e30), axis=-1, keepdims=True)
    weights = jnp.exp(jnp.where(allowed, scores - score_peak, -1e30))
    weight_total = jnp.sum(weights, axis=-1, keepdims=True)
    mixed_latent = (
        jnp.einsum(
            "qhk,kl->qhl",
            weights.astype(jnp.bfloat16),
            all_keys[:, :latent_width],
            preferred_element_type=jnp.float32,
        )
        / weight_total
    )
    mixed_latent = mixed_latent.astype(jnp.bfloat16)
    head_values = (
        jnp.einsum("qhl,hlv->qhv", mixed_latent, uv_weight, preferred_element_type=jnp.float32)
        .astype(jnp.bfloat16)
        .reshape(seq_rows, -1)
    )
    head_part = jnp.dot(head_values, out_weight, preferred_element_type=jnp.float32)
    attention = lax.psum(head_part, "exp")
    hidden = (local_rows.astype(jnp.float32) + attention).astype(jnp.bfloat16)
    normed = rms_scale(hidden.astype(jnp.float32), post_gain.astype(jnp.float32)).astype(
        jnp.bfloat16
    )
    logits = jnp.dot(normed, router_weight, preferred_element_type=jnp.float32)
    router_probs = jax.nn.softmax(logits, axis=-1)
    picked_ids = expert_ids[0]
    experts_all = router_weight.shape[1]
    top_count = picked_ids.shape[1]
    chosen = jnp.take_along_axis(router_probs, picked_ids, axis=1)
    chosen_sum = jnp.sum(chosen, axis=1, keepdims=True)
    route_w = chosen / chosen_sum
    route_wb = route_w.astype(jnp.bfloat16)
    ctx_count = lax.axis_size("ctx")
    held_experts = experts_all // ctx_count
    capacity = (4 * seq_rows * top_count + 3 * experts_all - 1) // (3 * experts_all)
    flat_ids = picked_ids.reshape(-1)
    onehot = (flat_ids[:, None] == jnp.arange(experts_all, dtype=jnp.int32)[None, :]).astype(
        jnp.int32
    )
    slot_rank = jnp.sum((jnp.cumsum(onehot, axis=0) - onehot) * onehot, axis=1).reshape(
        seq_rows, top_count
    )
    dp_count = lax.axis_size("dp")
    local_count = held_experts // dp_count
    first_local = lax.axis_index("dp") * local_count
    gate_local = lax.dynamic_slice_in_dim(gate_weight, first_local, local_count, 0)
    up_local = lax.dynamic_slice_in_dim(up_weight, first_local, local_count, 0)
    down_local = lax.dynamic_slice_in_dim(down_weight, first_local, local_count, 0)
    home_ctx = picked_ids // held_experts
    remainder = picked_ids % held_experts
    home_dp = remainder // local_count
    within = remainder % local_count
    slot_index = ((home_dp * ctx_count + home_ctx) * local_count + within) * capacity + slot_rank
    slot_hits = (
        slot_index[:, :, None] == jnp.arange(experts_all * capacity, dtype=jnp.int32)[None, None, :]
    )
    dispatch = jnp.any(slot_hits, axis=1).astype(jnp.bfloat16)
    combine = jnp.sum(
        jnp.where(slot_hits, route_wb[:, :, None], jnp.zeros((), jnp.bfloat16)), axis=1
    )
    outgoing = jnp.einsum("se,sd->ed", dispatch, normed, preferred_element_type=jnp.float32).astype(
        jnp.bfloat16
    )
    outgoing = outgoing.reshape(-1, local_count, capacity, model_width)
    arrived = route_slots(outgoing)
    gate_pre = jnp.einsum("sjcd,jdf->sjcf", arrived, gate_local, preferred_element_type=jnp.float32)
    up_pre = jnp.einsum("sjcd,jdf->sjcf", arrived, up_local, preferred_element_type=jnp.float32)
    activated = (jax.nn.silu(gate_pre) * up_pre).astype(jnp.bfloat16)
    expert_part = jnp.einsum(
        "sjcf,jfd->sjcd", activated, down_local, preferred_element_type=jnp.float32
    ).astype(jnp.bfloat16)
    returned = lax.all_to_all(expert_part, ("dp", "ctx"), split_axis=0, concat_axis=0, tiled=True)
    returned = returned.reshape(experts_all * capacity, model_width)
    moe_part = jnp.dot(combine, returned, preferred_element_type=jnp.float32)
    cot_rows = cotangent[0]
    cross_terms = jnp.einsum("sd,ed->se", cot_rows, returned, preferred_element_type=jnp.float32)
    dweight_part = jnp.take_along_axis(cross_terms, slot_index, axis=1)
    moe, dweight = lax.psum((moe_part, dweight_part), "exp")
    layer_out = (hidden.astype(jnp.float32) + moe).astype(jnp.bfloat16)
    mean_term = jnp.sum(dweight * route_w, axis=1, keepdims=True)
    dchosen = (dweight - mean_term) / chosen_sum
    id_hits = (
        picked_ids[:, :, None] == jnp.arange(experts_all, dtype=jnp.int32)[None, None, :]
    ).astype(jnp.float32)
    dprobs = jnp.sum(id_hits * dchosen[:, :, None], axis=1)
    dlogits = router_probs * (dprobs - jnp.sum(router_probs * dprobs, axis=1, keepdims=True))
    router_term = jnp.dot(normed.astype(jnp.float32).T, dlogits, precision=lax.Precision.HIGHEST)
    router_grad = lax.psum(router_term, ("dp", "ctx"))
    slot_cot = jnp.einsum(
        "se,sd->ed", combine, cot_rows, preferred_element_type=jnp.float32
    ).astype(jnp.bfloat16)
    slot_cot = slot_cot.reshape(-1, local_count, capacity, model_width)
    cot_arrived = route_slots(slot_cot)
    down_term = jnp.einsum(
        "sjcf,sjcd->jfd", activated, cot_arrived, preferred_element_type=jnp.float32
    )
    dact = jnp.einsum("sjcd,jfd->sjcf", cot_arrived, down_local, preferred_element_type=jnp.float32)
    sigmoid_gate = jax.nn.sigmoid(gate_pre)
    dgate = (dact * up_pre * sigmoid_gate * (1.0 + gate_pre * (1.0 - sigmoid_gate))).astype(
        jnp.bfloat16
    )
    dup = (dact * gate_pre * sigmoid_gate).astype(jnp.bfloat16)
    gate_term = jnp.einsum("sjcd,sjcf->jdf", arrived, dgate, preferred_element_type=jnp.float32)
    up_term = jnp.einsum("sjcd,sjcf->jdf", arrived, dup, preferred_element_type=jnp.float32)
    gate_out, up_out = in_one_piece(
        (gate_term.astype(jnp.bfloat16), up_term.astype(jnp.bfloat16)), "dp", 1, 0, 2
    )
    down_out = lax.all_to_all(
        down_term.astype(jnp.bfloat16), "dp", split_axis=2, concat_axis=0, tiled=True
    )
    return (layer_out[None], router_grad, gate_out, up_out, down_out)


def solution(mesh):
    placed = (
        P("dp", "ctx", None),
        P("dp", "ctx", "exp", None),
        P("exp", None),
        P(),
        P("exp", None, None),
        P("exp", None),
        P(),
        P(),
        P("dp", "ctx", None),
        P("dp", "ctx"),
        P("ctx", None, "exp"),
        P("ctx", None, "exp"),
        P("ctx", "exp", None),
        P("dp", "ctx", None),
    )
    return jax.shard_map(
        local,
        mesh=mesh,
        in_specs=placed,
        out_specs=(
            P("dp", "ctx", None),
            P(),
            P("ctx", "dp", "exp"),
            P("ctx", "dp", "exp"),
            P("ctx", "exp", "dp"),
        ),
        check_vma=False,
    )
```

profile of v0, /device:TPU:88, one launch (start us, length us, event | category | flops | bytes accessed | tf_op | source)
XLA Modules:
  0.0 998.6 jit_solution(10595866600486797685)
XLA Ops:
  10.4 5.8 all-to-all-start
  16.3 29.8 %all-to-all-done = f32[8,128,576]{1,2,0:T(8,128)} async-done(((f32[8,128,576]{1,2,0:T(8,128)}), f32[8,128,576]{1,2,0:T(8,128)}, u32[]{:S(2)}, u32[]{:S(2)}) %all-to-all-start) | async-done | bytes 2359328 | tf_op jit(solution)/shard_map/all_to_all | solution.py:13
  49.0 37.8 %all-gather = s32[1,2048]{1,0:T(1,128)S(1)} all-gather(s32[1,128]{1,0:T(1,128)S(1)} %copy-done.4), channel_id=2, replica_groups=mesh['dp'=2,'ctx'=16,'exp'=8] {'ctx'}, dimensions={1}, use_global_device_ids=true | all-gather | bytes 8704 | tf_op jit(solution)/shard_map/all_gather | solution.py:93
  87.1 26.5 %all-gather.3.cloned.1.call-done = bf16[2048,576]{0,1:T(8,128)(2,1)} async-done(((bf16[128,576]{0,1:T(8,128)(2,1)}), bf16[2048,576]{0,1:T(8,128)(2,1)}) %all-gather.3.cloned.1.call-update) | async-done | bytes 2359312 | tf_op jit(solution)/shard_map/all_gather | solution.py:92
  126.0 83.0 %all-reduce.4.cloned.1.call-done = f32[128,2560]{1,0:T(8,128)} async-done(((f32[128,2560]{1,0:T(8,128)}), f32[128,2560]{1,0:T(8,128)}) %all-reduce.4.cloned.1.call-update) | async-done | bytes 1310736 | tf_op jit(solution)/shard_map/psum | solution.py:124
  210.8 3.9 convolution_convert_fusion.2
  214.7 8.9 all-to-all-start.1
  223.7 113.3 %all-to-all-done.1 = bf16[32,1,32,2560]{3,2,1,0:T(8,128)(2,1)} async-done(((bf16[32,1,32,2560]{3,2,1,0:T(8,128)(2,1)}), bf16[32,1,32,2560]{3,2,1,0:T(8,128)(2,1)}, u32[]{:S(2)}, u32[]{:S(2)}) %all-to-all-start.1) | async-done | bytes 5242912 | tf_op jit(solution)/shard_map/all_to_all | solution.py:56
  336.9 4.4 fusion.55
  341.4 5.4 multiply_convert_fusion.2
  351.4 12.1 %all-to-all-start.2 = ((bf16[32,1,32,2560]{3,2,1,0:T(8,128)(2,1)}), bf16[32,1,32,2560]{3,2,1,0:T(8,128)(2,1)}, u32[]{:S(2)}, u32[]{:S(2)}) async-start(bf16[32,1,32,2560]{3,2,1,0:T(8,128)(2,1)} %fusion.13), calls=%async_computation.2 | async-start | bytes 10485760 | tf_op jit(solution)/shard_map/all_to_all | solution.py:177
  364.6 5.1 gather_fusion
  370.0 107.0 %all-to-all-done.2 = bf16[32,1,32,2560]{3,2,1,0:T(8,128)(2,1)} async-done(((bf16[32,1,32,2560]{3,2,1,0:T(8,128)(2,1)}), bf16[32,1,32,2560]{3,2,1,0:T(8,128)(2,1)}, u32[]{:S(2)}, u32[]{:S(2)}) %all-to-all-start.2) | async-done | bytes 5242912 | tf_op jit(solution)/shard_map/all_to_all | solution.py:177
  477.0 4.1 convolution_bitcast_fusion
  481.1 5.1 gather_fusion.1
  486.4 23.5 %psum.30 = f32[128,6]{0,1:T(8,128)S(1)} all-reduce(f32[128,6]{0,1:T(8,128)S(1)} %and_select_fusion), channel_id=1, replica_groups=mesh['dp'=2,'ctx'=16,'exp'=8] {'exp'}, use_global_device_ids=true, to_apply=%region_15.16 | all-reduce | flops 768 | bytes 6144 | tf_op jit(solution)/shard_map/psum | solution.py:183
  510.4 5.0 convolution_convert_fusion
  515.4 9.6 all-to-all-start.3
  525.0 4.4 fusion.159
  530.9 158.4 %all-reduce.6.cloned.1.call-done = f32[128,2560]{1,0:T(8,128)} async-done(((f32[128,2560]{1,0:T(8,128)}), f32[128,2560]{1,0:T(8,128)}) %all-reduce.6.cloned.1.call-update) | async-done | bytes 1310736 | tf_op jit(solution)/shard_map/psum | solution.py:183
  691.6 4.1 fusion.61
  695.8 3.9 fusion.38
  704.9 8.9 copy.117
  714.4 18.2 %reduce.3 = bf16[2560,384]{1,0:T(8,128)(2,1)} reduce(bf16[2560,1,384]{2,1,0:T(2,128)(2,1)} %bitcast.237, bf16[]{:T(256)} %broadcast.489), dimensions={1}, to_apply=%bitcast.212.reduce_sub_computation | reduce | bytes 3932162
  735.3 8.4 all_to_all.50
  743.7 4.2 reshape.426
  750.5 4.7 fusion.32
  760.5 6.3 copy.118
  766.8 15.4 %reduce.4 = bf16[2560,192]{1,0:T(8,128)(2,1)S(1)} reduce(bf16[2560,1,192]{2,1,0:T(2,128)(2,1)} %bitcast.241, bf16[]{:T(256)} %broadcast.489), dimensions={1}, to_apply=%bitcast.214.reduce_sub_computation | reduce | bytes 1966082
  784.5 5.6 all_to_all.51
  793.0 5.1 copy.119
  801.5 188.8 %all-reduce.8.cloned.1.call-done = f32[2560,32]{0,1:T(8,128)} async-done(((f32[2560,32]{0,1:T(8,128)}), f32[2560,32]{0,1:T(8,128)}) %all-reduce.8.cloned.1.call-update) | async-done | bytes 327696 | tf_op jit(solution)/shard_map/psum | solution.py:193
  (104 shorter events, 57.5 us)
Async XLA Ops:
  7.2 340.4 %copy-start = (bf16[2,192,2560]{2,1,0:T(8,128)(2,1)S(1)}, bf16[2,192,2560]{2,1,0:T(8,128)(2,1)}, u32[]{:S(2)}) copy-start(bf16[2,192,2560]{2,1,0:T(8,128)(2,1)} %param.26) | copy-start | bytes 5898244
  10.4 5.9 copy-start.5
  10.4 35.7 %all-to-all-start = ((f32[8,128,576]{1,2,0:T(8,128)}), f32[8,128,576]{1,2,0:T(8,128)}, u32[]{:S(2)}, u32[]{:S(2)}) async-start(f32[8,128,576]{1,2,0:T(8,128)} %broadcast_in_dim.34), calls=%async_computation | async-start | bytes 4718592 | tf_op jit(solution)/shard_map/all_to_all | solution.py:13
  16.1 32.8 %copy-start.4 = (s32[1,128]{1,0:T(1,128)S(1)}, s32[1,128]{1,0:T(1,128)}, u32[]{:S(2)}) copy-start(s32[1,128]{1,0:T(1,128)} %param.23) | copy-start | bytes 1540
  16.2 97.5 %copy-start.7 = (bf16[1,128,2,576]{1,3,2,0:T(8,128)(2,1)S(1)}, bf16[1,128,2,576]{1,3,2,0:T(8,128)(2,1)}, u32[]{:S(2)}) copy-start(bf16[1,128,2,576]{1,3,2,0:T(8,128)(2,1)} %param.15) | copy-start | bytes 884740
  16.2 97.4 %all-gather.3.cloned.1.call-start = ((), (), s32[]{:S(2)}) async-start(), calls=%async_computation.6 | async-start | bytes 2506752 | tf_op jit(solution)/shard_map/all_gather | solution.py:92
  48.9 160.1 %all-reduce.4.cloned.1.call-start = ((), (), s32[]{:S(2)}) async-start(), calls=%async_computation.7 | async-start | bytes 2621440 | tf_op jit(solution)/shard_map/psum | solution.py:124
  118.3 2.9 copy-start.1
  121.2 1.5 copy-start.2
  121.2 4.3 copy-start.3
  214.7 122.2 %all-to-all-start.1 = ((bf16[32,1,32,2560]{3,2,1,0:T(8,128)(2,1)}), bf16[32,1,32,2560]{3,2,1,0:T(8,128)(2,1)}, u32[]{:S(2)}, u32[]{:S(2)}) async-start(bf16[32,1,32,2560]{3,2,1,0:T(8,128)(2,1)} %bitcast.235), calls=%async_computation.1 | async-start | bytes 10485760 | tf_op jit(solution)/shard_map/all_to_all | solution.py:56
  336.9 4.5 copy-start.6
  341.4 5.4 copy-start.9
  346.8 0.8 copy-start.12
  351.4 12.7 %copy-start.8 = (bf16[2560,32]{0,1:T(8,128)(2,1)S(1)}, bf16[2560,32]{0,1:T(8,128)(2,1)}, u32[]{:S(2)}) copy-start(bf16[2560,32]{0,1:T(8,128)(2,1)} %param.21) | copy-start | bytes 491524
  351.4 125.5 %all-to-all-start.2 = ((bf16[32,1,32,2560]{3,2,1,0:T(8,128)(2,1)}), bf16[32,1,32,2560]{3,2,1,0:T(8,128)(2,1)}, u32[]{:S(2)}, u32[]{:S(2)}) async-start(bf16[32,1,32,2560]{3,2,1,0:T(8,128)(2,1)} %fusion.13), calls=%async_computation.2 | async-start | bytes 10485760 | tf_op jit(solution)/shard_map/all_to_all | solution.py:177
  515.4 176.2 %all-to-all-start.3 = ((bf16[32,1,32,2560]{3,2,1,0:T(8,128)(2,1)}), bf16[32,1,32,2560]{3,2,1,0:T(8,128)(2,1)}, u32[]{:S(2)}, u32[]{:S(2)}) async-start(bf16[32,1,32,2560]{3,2,1,0:T(8,128)(2,1)} %bitcast.236), calls=%async_computation.3 | async-start | bytes 10485760 | tf_op jit(solution)/shard_map/all_to_all | solution.py:56
  525.0 164.4 %all-reduce.6.cloned.1.call-start = ((), (), s32[]{:S(2)}) async-start(), calls=%async_computation.8 | async-start | bytes 2621440 | tf_op jit(solution)/shard_map/psum | solution.py:183
  529.4 460.9 %all-reduce.8.cloned.1.call-start = ((), (), s32[]{:S(2)}) async-start(), calls=%async_computation.9 | async-start | bytes 655360 | tf_op jit(solution)/shard_map/psum | solution.py:193
  691.6 4.1 copy-start.10
  695.8 3.9 copy-start.11
  748.0 2.5 copy-start.13
Sparse Core Ops, SparseCore 0:
  49.1 64.4 all-gather.2
  122.8 86.1 all-reduce.3
  529.6 159.7 all-reduce.5
  692.4 297.9 all-reduce.7
where the time goes:
time: 1000 us; the launch traced here: 999 us
  waiting for transfers between devices  707 us (71%)
  blocking collectives  75.3 us (8%)
  local copies, waits for them, and re-layouts  60.3 us (6%)
  matrix products  58.1 us (6%)
  other arithmetic  47.3 us (5%)
  starting transfers between devices  36.6 us (4%)
  between operations  14.2 us (1%)
    psum x1, waiting for transfers between devices, local(): router_grad = lax.psum(router_term, ('dp', 'ctx'))  189 us
    psum x1, waiting for transfers between devices, local(): moe, dweight = lax.psum((moe_part, dweight_part), 'exp')  158 us
    all_to_all x2, waiting for transfers between devices, route_slots(): lax.all_to_all(outgoing, ('dp', 'ctx'), split_axis=0, concat_axis=0, tile...  113 us
    all_to_all x1, waiting for transfers between devices, local(): lax.all_to_all(expert_part, ('dp', 'ctx'), split_axis=0, concat_axis=0, t...  107 us
    psum x1, waiting for transfers between devices, local(): attention = lax.psum(head_part, 'exp')  83 us
    all_gather x1, blocking collectives, local(): lax.all_gather(doc_ids[0], 'ctx', axis=0, tiled=True)  37.8 us
    unnamed x2, other arithmetic  33.5 us
    all_to_all x1, waiting for transfers between devices, from_everyone(): lax.all_to_all(jnp.broadcast_to(array[None], (count, *array.shape)), axis...  29.8 us
  transfers between devices with their start and end apart: 8, of which 7 were waited for; matrix products, arithmetic and copies ran while one was open for 11% of the time, Pallas kernels for 0%

commit v1 on v0

--- a/solution.py
+++ b/solution.py
@@ -190,7 +190,7 @@
     dprobs = jnp.sum(id_hits * dchosen[:, :, None], axis=1)
     dlogits = router_probs * (dprobs - jnp.sum(router_probs * dprobs, axis=1, keepdims=True))
     router_term = jnp.dot(normed.astype(jnp.float32).T, dlogits, precision=lax.Precision.HIGHEST)
-    router_grad = lax.psum(router_term, ("dp", "ctx"))
+    router_grad = lax.psum(lax.psum(router_term, "dp"), "ctx")
     slot_cot = jnp.einsum(
         "se,sd->ed", combine, cot_rows, preferred_element_type=jnp.float32
     ).astype(jnp.bfloat16)

time: 1000 us -> 876 us (0.88)
  waiting for transfers between devices: 707 us -> 581 us
    psum x1 -> x2, waiting for transfers between devices: 189 us -> 77.1 us  [local(): router_grad = lax.psum(lax.psum(router_term, 'dp'), 'ctx')]
    psum x1, waiting for transfers between devices: 158 us -> 144 us  [local(): moe, dweight = lax.psum((moe_part, dweight_part), 'exp')]
  transfers between devices with their start and end apart: 8 -> 9, of which waited for: 7 -> 8; matrix products, arithmetic and copies ran while one was open for 11% -> 13% of each run, Pallas kernels for 0% -> 0%
where the time goes in v1:
time: 876 us; the launch traced here: 873 us
  waiting for transfers between devices  581 us (66%)
  blocking collectives  75.3 us (9%)
  local copies, waits for them, and re-layouts  60.3 us (7%)
  matrix products  58.1 us (7%)
  other arithmetic  47.4 us (5%)
  starting transfers between devices  36.6 us (4%)
  between operations  14.3 us (2%)
    psum x1, waiting for transfers between devices, local(): moe, dweight = lax.psum((moe_part, dweight_part), 'exp')  144 us
    all_to_all x2, waiting for transfers between devices, route_slots(): lax.all_to_all(outgoing, ('dp', 'ctx'), split_axis=0, concat_axis=0, tile...  113 us
    all_to_all x1, waiting for transfers between devices, local(): lax.all_to_all(expert_part, ('dp', 'ctx'), split_axis=0, concat_axis=0, t...  107 us
    psum x1, waiting for transfers between devices, local(): attention = lax.psum(head_part, 'exp')  83 us
    psum x2, waiting for transfers between devices, local(): router_grad = lax.psum(lax.psum(router_term, 'dp'), 'ctx')  77.1 us
    all_gather x1, blocking collectives, local(): lax.all_gather(doc_ids[0], 'ctx', axis=0, tiled=True)  37.8 us
    unnamed x2, other arithmetic  33.6 us
    all_to_all x1, waiting for transfers between devices, from_everyone(): lax.all_to_all(jnp.broadcast_to(array[None], (count, *array.shape)), axis...  29.8 us
  transfers between devices with their start and end apart: 9, of which 8 were waited for; matrix products, arithmetic and copies ran while one was open for 13% of the time, Pallas kernels for 0%

profile of v1, /device:TPU:88, one launch (start us, length us, event | category | flops | bytes accessed | tf_op | source)
XLA Modules:
  0.0 872.5 jit_solution(17468212148804864995)
XLA Ops:
  10.4 5.8 all-to-all-start
  16.3 29.8 %all-to-all-done = f32[8,128,576]{1,2,0:T(8,128)} async-done(((f32[8,128,576]{1,2,0:T(8,128)}), f32[8,128,576]{1,2,0:T(8,128)}, u32[]{:S(2)}, u32[]{:S(2)}) %all-to-all-start) | async-done | bytes 2359328 | tf_op jit(solution)/shard_map/all_to_all | solution.py:13
  49.0 37.8 %all-gather = s32[1,2048]{1,0:T(1,128)S(1)} all-gather(s32[1,128]{1,0:T(1,128)S(1)} %copy-done.4), channel_id=2, replica_groups=mesh['dp'=2,'ctx'=16,'exp'=8] {'ctx'}, dimensions={1}, use_global_device_ids=true | all-gather | bytes 8704 | tf_op jit(solution)/shard_map/all_gather | solution.py:93
  87.1 26.5 %all-gather.3.cloned.1.call-done = bf16[2048,576]{0,1:T(8,128)(2,1)} async-done(((bf16[128,576]{0,1:T(8,128)(2,1)}), bf16[2048,576]{0,1:T(8,128)(2,1)}) %all-gather.3.cloned.1.call-update) | async-done | bytes 2359312 | tf_op jit(solution)/shard_map/all_gather | solution.py:92
  126.0 83.0 %all-reduce.5.cloned.1.call-done = f32[128,2560]{1,0:T(8,128)} async-done(((f32[128,2560]{1,0:T(8,128)}), f32[128,2560]{1,0:T(8,128)}) %all-reduce.5.cloned.1.call-update) | async-done | bytes 1310736 | tf_op jit(solution)/shard_map/psum | solution.py:124
  210.8 3.9 convolution_convert_fusion.2
  214.7 8.9 %all-to-all-start.1 = ((bf16[32,1,32,2560]{3,2,1,0:T(8,128)(2,1)}), bf16[32,1,32,2560]{3,2,1,0:T(8,128)(2,1)}, u32[]{:S(2)}, u32[]{:S(2)}) async-start(bf16[32,1,32,2560]{3,2,1,0:T(8,128)(2,1)} %bitcast.235), calls=%async_computation.1 | async-start | bytes 10485760 | tf_op jit(solution)/shard_map/all_to_all | solution.py:56
  223.7 113.3 %all-to-all-done.1 = bf16[32,1,32,2560]{3,2,1,0:T(8,128)(2,1)} async-done(((bf16[32,1,32,2560]{3,2,1,0:T(8,128)(2,1)}), bf16[32,1,32,2560]{3,2,1,0:T(8,128)(2,1)}, u32[]{:S(2)}, u32[]{:S(2)}) %all-to-all-start.1) | async-done | bytes 5242912 | tf_op jit(solution)/shard_map/all_to_all | solution.py:56
  336.9 4.4 fusion.55
  341.4 5.4 multiply_convert_fusion.2
  351.4 12.1 %all-to-all-start.2 = ((bf16[32,1,32,2560]{3,2,1,0:T(8,128)(2,1)}), bf16[32,1,32,2560]{3,2,1,0:T(8,128)(2,1)}, u32[]{:S(2)}, u32[]{:S(2)}) async-start(bf16[32,1,32,2560]{3,2,1,0:T(8,128)(2,1)} %fusion.13), calls=%async_computation.2 | async-start | bytes 10485760 | tf_op jit(solution)/shard_map/all_to_all | solution.py:177
  364.6 5.1 gather_fusion
  370.0 107.0 %all-to-all-done.2 = bf16[32,1,32,2560]{3,2,1,0:T(8,128)(2,1)} async-done(((bf16[32,1,32,2560]{3,2,1,0:T(8,128)(2,1)}), bf16[32,1,32,2560]{3,2,1,0:T(8,128)(2,1)}, u32[]{:S(2)}, u32[]{:S(2)}) %all-to-all-start.2) | async-done | bytes 5242912 | tf_op jit(solution)/shard_map/all_to_all | solution.py:177
  477.0 4.1 convolution_bitcast_fusion
  481.1 5.1 gather_fusion.1
  486.4 23.5 %psum.37 = f32[128,6]{0,1:T(8,128)S(1)} all-reduce(f32[128,6]{0,1:T(8,128)S(1)} %and_select_fusion), channel_id=1, replica_groups=mesh['dp'=2,'ctx'=16,'exp'=8] {'exp'}, use_global_device_ids=true, to_apply=%region_15.16 | all-reduce | flops 768 | bytes 6144 | tf_op jit(solution)/shard_map/psum | solution.py:183
  510.4 5.0 convolution_convert_fusion
  515.4 9.6 %all-to-all-start.3 = ((bf16[32,1,32,2560]{3,2,1,0:T(8,128)(2,1)}), bf16[32,1,32,2560]{3,2,1,0:T(8,128)(2,1)}, u32[]{:S(2)}, u32[]{:S(2)}) async-start(bf16[32,1,32,2560]{3,2,1,0:T(8,128)(2,1)} %bitcast.236), calls=%async_computation.3 | async-start | bytes 10485760 | tf_op jit(solution)/shard_map/all_to_all | solution.py:56
  526.4 4.4 fusion.159
  530.9 25.9 %all-reduce.9.cloned.1.call-done = f32[2560,32]{0,1:T(8,128)} async-done(((f32[2560,32]{0,1:T(8,128)}), f32[2560,32]{0,1:T(8,128)}) %all-reduce.9.cloned.1.call-update) | async-done | bytes 327696 | tf_op jit(solution)/shard_map/psum | solution.py:193
  556.9 143.9 %all-reduce.7.cloned.1.call-done = f32[128,2560]{1,0:T(8,128)} async-done(((f32[128,2560]{1,0:T(8,128)}), f32[128,2560]{1,0:T(8,128)}) %all-reduce.7.cloned.1.call-update) | async-done | bytes 1310736 | tf_op jit(solution)/shard_map/psum | solution.py:183
  703.1 4.1 fusion.61
  716.4 8.9 %copy.117 = bf16[1,2560,384]{2,0,1:T(2,128)(2,1)} copy(bf16[1,2560,384]{1,2,0:T(8,128)(2,1)} %pad_maximum_fusion) | data formatting | bytes 3932160 | tf_op jit(solution)/shard_map/concatenate | solution.py:24
  725.8 18.2 %reduce.3 = bf16[2560,384]{1,0:T(8,128)(2,1)} reduce(bf16[2560,1,384]{2,1,0:T(2,128)(2,1)} %bitcast.237, bf16[]{:T(256)} %broadcast.489), dimensions={1}, to_apply=%bitcast.212.reduce_sub_computation | reduce | bytes 3932162
  746.8 8.4 all_to_all.50
  755.2 4.2 reshape.426
  761.9 4.7 fusion.32
  771.9 6.3 copy.118
  778.2 15.4 %reduce.4 = bf16[2560,192]{1,0:T(8,128)(2,1)S(1)} reduce(bf16[2560,1,192]{2,1,0:T(2,128)(2,1)} %bitcast.241, bf16[]{:T(256)} %broadcast.489), dimensions={1}, to_apply=%bitcast.214.reduce_sub_computation | reduce | bytes 1966082
  796.0 5.6 all_to_all.51
  804.5 5.1 copy.119
  813.0 51.2 %all-reduce.11.cloned.1.call-done = f32[2560,32]{0,1:T(8,128)} async-done(((f32[2560,32]{0,1:T(8,128)}), f32[2560,32]{0,1:T(8,128)}) %all-reduce.11.cloned.1.call-update) | async-done | bytes 327696 | tf_op jit(solution)/shard_map/psum | solution.py:193
  (107 shorter events, 61.4 us)
Async XLA Ops:
  7.2 340.4 %copy-start = (bf16[2,192,2560]{2,1,0:T(8,128)(2,1)S(1)}, bf16[2,192,2560]{2,1,0:T(8,128)(2,1)}, u32[]{:S(2)}) copy-start(bf16[2,192,2560]{2,1,0:T(8,128)(2,1)} %param.26) | copy-start | bytes 5898244
  10.4 5.9 copy-start.5
  10.4 35.7 %all-to-all-start = ((f32[8,128,576]{1,2,0:T(8,128)}), f32[8,128,576]{1,2,0:T(8,128)}, u32[]{:S(2)}, u32[]{:S(2)}) async-start(f32[8,128,576]{1,2,0:T(8,128)} %broadcast_in_dim.34), calls=%async_computation | async-start | bytes 4718592 | tf_op jit(solution)/shard_map/all_to_all | solution.py:13
  16.1 32.8 %copy-start.4 = (s32[1,128]{1,0:T(1,128)S(1)}, s32[1,128]{1,0:T(1,128)}, u32[]{:S(2)}) copy-start(s32[1,128]{1,0:T(1,128)} %param.23) | copy-start | bytes 1540
  16.2 97.5 %copy-start.7 = (bf16[1,128,2,576]{1,3,2,0:T(8,128)(2,1)S(1)}, bf16[1,128,2,576]{1,3,2,0:T(8,128)(2,1)}, u32[]{:S(2)}) copy-start(bf16[1,128,2,576]{1,3,2,0:T(8,128)(2,1)} %param.15) | copy-start | bytes 884740
  16.2 97.4 %all-gather.3.cloned.1.call-start = ((), (), s32[]{:S(2)}) async-start(), calls=%async_computation.6 | async-start | bytes 2506752 | tf_op jit(solution)/shard_map/all_gather | solution.py:92
  48.9 160.1 %all-reduce.5.cloned.1.call-start = ((), (), s32[]{:S(2)}) async-start(), calls=%async_computation.7 | async-start | bytes 2621440 | tf_op jit(solution)/shard_map/psum | solution.py:124
  118.3 2.9 copy-start.1
  121.2 1.5 copy-start.2
  121.2 4.3 copy-start.3
  214.7 122.2 %all-to-all-start.1 = ((bf16[32,1,32,2560]{3,2,1,0:T(8,128)(2,1)}), bf16[32,1,32,2560]{3,2,1,0:T(8,128)(2,1)}, u32[]{:S(2)}, u32[]{:S(2)}) async-start(bf16[32,1,32,2560]{3,2,1,0:T(8,128)(2,1)} %bitcast.235), calls=%async_computation.1 | async-start | bytes 10485760 | tf_op jit(solution)/shard_map/all_to_all | solution.py:56
  336.9 4.5 copy-start.6
  341.4 5.4 copy-start.9
  346.8 0.8 copy-start.12
  351.4 12.7 %copy-start.8 = (bf16[2560,32]{0,1:T(8,128)(2,1)S(1)}, bf16[2560,32]{0,1:T(8,128)(2,1)}, u32[]{:S(2)}) copy-start(bf16[2560,32]{0,1:T(8,128)(2,1)} %param.21) | copy-start | bytes 491524
  351.4 125.5 %all-to-all-start.2 = ((bf16[32,1,32,2560]{3,2,1,0:T(8,128)(2,1)}), bf16[32,1,32,2560]{3,2,1,0:T(8,128)(2,1)}, u32[]{:S(2)}, u32[]{:S(2)}) async-start(bf16[32,1,32,2560]{3,2,1,0:T(8,128)(2,1)} %fusion.13), calls=%async_computation.2 | async-start | bytes 10485760 | tf_op jit(solution)/shard_map/all_to_all | solution.py:177
  515.4 187.7 %all-to-all-start.3 = ((bf16[32,1,32,2560]{3,2,1,0:T(8,128)(2,1)}), bf16[32,1,32,2560]{3,2,1,0:T(8,128)(2,1)}, u32[]{:S(2)}, u32[]{:S(2)}) async-start(bf16[32,1,32,2560]{3,2,1,0:T(8,128)(2,1)} %bitcast.236), calls=%async_computation.3 | async-start | bytes 10485760 | tf_op jit(solution)/shard_map/all_to_all | solution.py:56
  525.0 31.9 %all-reduce.9.cloned.1.call-start = ((), (), s32[]{:S(2)}) async-start(), calls=%async_computation.9 | async-start | bytes 655360 | tf_op jit(solution)/shard_map/psum | solution.py:193
  526.4 174.4 %all-reduce.7.cloned.1.call-start = ((), (), s32[]{:S(2)}) async-start(), calls=%async_computation.8 | async-start | bytes 2621440 | tf_op jit(solution)/shard_map/psum | solution.py:183
  530.9 333.4 %all-reduce.11.cloned.1.call-start = ((), (), s32[]{:S(2)}) async-start(), calls=%async_computation.10 | async-start | bytes 655360 | tf_op jit(solution)/shard_map/psum | solution.py:193
  703.1 4.1 copy-start.10
  707.2 3.9 copy-start.11
  759.4 2.5 copy-start.13
Sparse Core Ops, SparseCore 0:
  49.1 64.4 all-gather.2
  122.8 86.1 all-reduce.4
  528.9 27.8 all-reduce.8
  559.3 141.3 all-reduce.6
  703.2 160.9 all-reduce.10
